TPU v7x, 32 devices: a whole 2x2x4 slice. The times are simulated.
32 devices in a mesh: geom: 2 (over x), op: 8 (over z, y), col: 2 (over core).
Axes of the slice: x: 2, y: 2, z: 4, core: 2. Of those that a mesh axis runs over, the one named last changes fastest.
Arguments:
- wave_coef: float32 [2048, 1024], P('geom', 'col'), parts along dimension 0, may hold values from -6 to 6
- diag_energy: float32 [2048, 1024], P('geom', 'col'), parts along dimension 0, may hold values from -4 to 4
- left_block: bfloat16 [32, 1024, 1024], P(('geom', 'op')), parts along dimension 0, may hold values from -0.1875 to 0.1875
- right_block: bfloat16 [32, 1024, 1024], P(('geom', 'op'), None, 'col'), parts along dimension 0, may hold values from -0.1875 to 0.1875
- block_mask: int32 [32, 8, 8], P(('geom', 'op')), parts along dimension 0, may hold values 0 or 1
Outputs:
- new_wave: float32 [2048, 1024], P('geom', 'col'), parts along dimension 0
There are 2 independent parts, one for each index of `geom`. A program takes and returns all parts, laid end to end along the dimension named above; each array names one. Nothing has to cross between parts.
All inputs are finite; a program needn't handle non-finite values. No bound on the sum of `block_mask` on one device may be relied on, other than what follows from the above.
Results may differ from a plain program's by a relative error of at most 0.0042.
The roundings to bfloat16 on the way count: a program that leaves them out, or rounds other values in their place, can miss the bound.
Values may be sent and summed in bfloat16 or wider, within the bound.
A program may use at most 64 MiB of HBM per device.

v0:
```python
import jax
import jax.numpy as jnp
from jax import lax
from jax.sharding import PartitionSpec as P

M = 1024
STEPS = 2


def apply_mask(left_block, block_mask):
    total, width, _ = left_block.shape
    blocks = block_mask.shape[1]
    inside = width // blocks
    grid = left_block.reshape(total, blocks, inside, blocks, inside)
    keep = block_mask.astype(jnp.bfloat16)[:, :, None, :, None]
    return (grid * keep).reshape(total, width, width)


def correct(coef, sigma, diag_energy, correlation, weight, cells):
    theta = correlation / cells / (weight / cells + 1e-06)
    spacing = diag_energy - theta
    correction = (sigma - theta * coef) * spacing / jnp.maximum(spacing * spacing, 1.0)
    return coef - correction


def update_cols(coef, sigma, diag_energy, cells):
    correlation, weight = lax.psum((jnp.sum(coef * sigma), jnp.sum(coef * coef)), "col")
    moved = correct(coef, sigma, diag_energy, correlation, weight, cells)
    norm_sum = lax.psum(jnp.sum(moved * moved), "col")
    return moved * lax.rsqrt(norm_sum / cells + 1e-06)


def local(wave_coef, diag_energy, left_block, right_block, block_mask):
    masked = apply_mask(left_block, block_mask)
    cells = float(M * M)
    coef = wave_coef
    wave = wave_coef.astype(jnp.bfloat16)
    for step in range(STEPS):
        wave = coef.astype(jnp.bfloat16)
        inner = jnp.einsum(
            "mj,kjc->kmc",
            lax.all_gather(wave, "col", axis=1, tiled=True),
            right_block,
            preferred_element_type=jnp.float32,
        ).astype(jnp.bfloat16)
        partial_sum = jnp.einsum("kab,kbc->ac", masked, inner, preferred_element_type=jnp.float32)
        sigma = lax.psum(partial_sum, "op")
        coef = update_cols(coef, sigma, diag_energy, cells)
    return coef


def solution(mesh):
    in_specs = (
        P("geom", "col"),
        P("geom", "col"),
        P(("geom", "op"), None, None),
        P(("geom", "op"), None, "col"),
        P(("geom", "op"), None, None),
    )
    out_specs = P("geom", "col")
    return jax.shard_map(local, mesh=mesh, in_specs=in_specs, out_specs=out_specs, check_vma=False)
```

profile of v0, /device:TPU:0, one launch (start us, length us, event | category | flops | bytes accessed | tf_op | source)
XLA Modules:
  0.0 310.1 jit_solution(6017176165767036142)
XLA Ops:
  6.5 0.0 copy-start
  6.5 0.0 copy-start.1
  6.5 0.0 all-gather.3.cloned.1.call-start
  6.5 2.9 convert_element_type.22
  9.4 0.0 all-gather.3.cloned.1.call-update
  9.4 0.0 all-reduce.5.cloned.1.call-start
  9.5 0.0 copy-done.1
  9.5 2.5 mul.65
  12.0 7.4 %mul.66 = bf16[2,1024,1024]{2,1,0:T(8,128)(2,1)} reshape(bf16[2,8,128,8,128]{4,3,2,1,0:T(8,128)(2,1)} %mul.65) | data formatting | bytes 8388608 | tf_op jit(solution)/shard_map/mul | solution.py:16
  19.4 8.1 %mul.67 = bf16[2,1024,1024]{2,1,0:T(8,128)(2,1)} multiply(bf16[2,1024,1024]{2,1,0:T(8,128)(2,1)} %param.7, bf16[2,1024,1024]{2,1,0:T(8,128)(2,1)} %mul.66) | non-fusion elementwise | flops 2097152 | bytes 12582912 | tf_op jit(solution)/shard_map/mul | solution.py:16
  27.5 0.0 all-gather.3.cloned.1.call-done
  27.5 0.0 copy-done
  27.5 8.7 %fusion.10 = f32[1024,512]{1,0:T(8,128)} fusion(bf16[2,1024,1024]{2,1,0:T(8,128)(2,1)} %mul.67, bf16[2,1024,512]{2,1,0:T(8,128)(2,1)S(1)} %copy-done, bf16[1024,1024]{1,0:T(8,128)(2,1)} %all-gather.3.cloned.1.call-done), kind=kOutput, calls=%fused_computation.19 | convolution fusion | flops 4296015872 | bytes 10485760 | tf_op jit(solution)/shard_map/kab,kbc->ac/dot_general | solution.py:46
  36.1 0.0 all-reduce.5.cloned.1.call-update
  36.2 0.0 all-gather.5.cloned.1.call-start
  36.2 104.7 %all-reduce.5.cloned.1.call-done = f32[1024,512]{1,0:T(8,128)} async-done(((f32[1024,512]{1,0:T(8,128)}), f32[1024,512]{1,0:T(8,128)}) %all-reduce.5.cloned.1.call-update) | async-done | bytes 2097168 | tf_op jit(solution)/shard_map/psum | solution.py:47
  140.9 3.4 %multiply_reduce_fusion.4 = (f32[]{:T(128)}, f32[]{:T(128)}) fusion(f32[1024,512]{1,0:T(8,128)} %param.5, f32[1024,512]{1,0:T(8,128)} %all-reduce.5.cloned.1.call-done), kind=kLoop, calls=%fused_computation.15 | loop fusion | flops 2097150 | bytes 4194312 | tf_op jit(solution)/shard_map/reduce_sum | solution.py:27
  144.3 3.1 %all-reduce.1 = (f32[]{:T(128)}, f32[]{:T(128)}) all-reduce(f32[]{:T(128)} %get-tuple-element.8, f32[]{:T(128)} %get-tuple-element.7), channel_id=1, replica_groups=mesh['geom'=2,'op'=8,'col'=2] {'col'}, use_global_device_ids=true, to_apply=%region_2.0 | all-reduce | flops 2 | bytes 16 | tf_op jit(solution)/shard_map/psum | solution.py:27
  148.7 5.6 %multiply_reduce_fusion.3 = (f32[]{:T(128)}, f32[1024,512]{1,0:T(8,128)}) fusion(f32[1024,512]{1,0:T(8,128)} %param.5, f32[1024,512]{1,0:T(8,128)} %param.6, f32[1024,512]{1,0:T(8,128)} %all-reduce.5.cloned.1.call-done, f32[]{:T(128)S(6)} %div.32), kind=kLoop, calls=%fused_computation.13 | loop fusion | flops 5242879 | bytes 8388616 | tf_op jit(solution)/shard_map/reduce_sum | solution.py:29
  154.3 3.1 %psum.59 = f32[]{:T(128)} all-reduce(f32[]{:T(128)} %get-tuple-element.15), channel_id=1, replica_groups=mesh['geom'=2,'op'=8,'col'=2] {'col'}, use_global_device_ids=true, to_apply=%region_6.0 | all-reduce | flops 1 | bytes 8 | tf_op jit(solution)/shard_map/psum | solution.py:29
  158.1 2.8 multiply_convert_fusion
  160.9 0.0 all-gather.5.cloned.1.call-update
  160.9 0.0 all-reduce.7.cloned.1.call-start
  161.0 10.0 %all-gather.5.cloned.1.call-done = bf16[1024,1024]{1,0:T(8,128)(2,1)} async-done(((bf16[1024,512]{1,0:T(8,128)(2,1)}), bf16[1024,1024]{1,0:T(8,128)(2,1)}) %all-gather.5.cloned.1.call-update) | async-done | bytes 2097168 | tf_op jit(solution)/shard_map/all_gather | solution.py:42
  170.9 8.6 %fusion.13 = f32[1024,512]{1,0:T(8,128)} fusion(bf16[2,1024,1024]{2,1,0:T(8,128)(2,1)} %mul.67, bf16[2,1024,512]{2,1,0:T(8,128)(2,1)S(1)} %copy-done, bf16[1024,1024]{1,0:T(8,128)(2,1)} %all-gather.5.cloned.1.call-done), kind=kOutput, calls=%fused_computation.20 | convolution fusion | flops 4296015872 | bytes 10485760 | tf_op jit(solution)/shard_map/kab,kbc->ac/dot_general | solution.py:46
  179.6 0.0 all-reduce.7.cloned.1.call-update
  179.6 103.6 %all-reduce.7.cloned.1.call-done = f32[1024,512]{1,0:T(8,128)} async-done(((f32[1024,512]{1,0:T(8,128)}), f32[1024,512]{1,0:T(8,128)}) %all-reduce.7.cloned.1.call-update) | async-done | bytes 2097168 | tf_op jit(solution)/shard_map/psum | solution.py:47
  283.2 3.4 %multiply_reduce_fusion.1 = (f32[]{:T(128)}, f32[]{:T(128)}) fusion(f32[1024,512]{1,0:T(8,128)} %get-tuple-element.16, f32[]{:T(128)S(6)} %rsqrt.6, f32[1024,512]{1,0:T(8,128)} %all-reduce.7.cloned.1.call-done), kind=kLoop, calls=%fused_computation.10 | loop fusion | flops 2621438 | bytes 4194316 | tf_op jit(solution)/shard_map/reduce_sum | solution.py:27
  286.6 3.1 all-reduce
  290.9 5.6 %multiply_reduce_fusion = (f32[]{:T(128)}, f32[1024,512]{1,0:T(8,128)}) fusion(f32[1024,512]{1,0:T(8,128)} %param.6, f32[1024,512]{1,0:T(8,128)} %all-reduce.7.cloned.1.call-done, f32[]{:T(128)S(6)} %div.37, f32[1024,512]{1,0:T(8,128)} %get-tuple-element.16, f32[]{:T(128)S(6)} %rsqrt.6), kind=kLoop, calls=%fused_computation.8 | loop fusion | flops 5767167 | bytes 8388620 | tf_op jit(solution)/shard_map/reduce_sum | solution.py:29
  296.5 3.2 %psum.63 = f32[]{:T(128)} all-reduce(f32[]{:T(128)} %get-tuple-element.13), channel_id=1, replica_groups=mesh['geom'=2,'op'=8,'col'=2] {'col'}, use_global_device_ids=true, to_apply=%region_13.0 | all-reduce | flops 1 | bytes 8 | tf_op jit(solution)/shard_map/psum | solution.py:29
  300.4 3.1 %broadcast_multiply_fusion = f32[1024,512]{1,0:T(8,128)} fusion(f32[1024,512]{1,0:T(8,128)} %get-tuple-element.14, f32[]{:T(128)S(6)} %rsqrt.7), kind=kLoop, calls=%fused_computation.21 | loop fusion | flops 524288 | bytes 4194308 | tf_op jit(solution)/shard_map/mul | solution.py:30
  (1 shorter events, 0.0 us)
Async XLA Ops:
  6.5 20.9 %copy-start = (bf16[2,1024,512]{2,1,0:T(8,128)(2,1)S(1)}, bf16[2,1024,512]{2,1,0:T(8,128)(2,1)}, u32[]{:S(2)}) copy-start(bf16[2,1024,512]{2,1,0:T(8,128)(2,1)} %param.8) | copy-start | bytes 6291460
  6.5 2.9 copy-start.1
  6.5 20.9 %all-gather.3.cloned.1.call-start = ((), (), s32[]{:S(2)}) async-start(), calls=%async_computation | async-start | bytes 3145728 | tf_op jit(solution)/shard_map/all_gather | solution.py:42
  9.4 131.5 %all-reduce.5.cloned.1.call-start = ((), (), s32[]{:S(2)}) async-start(), calls=%async_computation.1 | async-start | bytes 4194304 | tf_op jit(solution)/shard_map/psum | solution.py:47
  36.2 134.8 %all-gather.5.cloned.1.call-start = ((), (), s32[]{:S(2)}) async-start(), calls=%async_computation.2 | async-start | bytes 3145728 | tf_op jit(solution)/shard_map/all_gather | solution.py:42
  160.9 122.3 %all-reduce.7.cloned.1.call-start = ((), (), s32[]{:S(2)}) async-start(), calls=%async_computation.3 | async-start | bytes 4194304 | tf_op jit(solution)/shard_map/psum | solution.py:47
Sparse Core Ops, SparseCore 0:
  9.5 13.2 all-gather.2
  36.3 104.5 all-reduce.4
  161.0 9.8 all-gather.4
  179.7 103.4 all-reduce.6
where the time goes:
time: 311 us; the launch traced here: 310 us
  waiting for transfers between devices  218 us (70%)
  other arithmetic  34.9 us (11%)
  matrix products  17.3 us (6%)
  between operations  17 us (5%)
  blocking collectives  12.5 us (4%)
  local copies, waits for them, and re-layouts  9.93 us (3%)
    psum x2, waiting for transfers between devices, local(): sigma = lax.psum(partial_sum, 'op')  208 us
    dot_general x2, matrix products, local(): jnp.einsum('kab,kbc->ac', masked, inner, preferred_element_type=jnp.float32)  17.3 us
    reduce_sum x2, other arithmetic, update_cols(): norm_sum = lax.psum(jnp.sum(moved * moved), 'col')  11.2 us
    all_gather x2, waiting for transfers between devices, local(): lax.all_gather(wave, 'col', axis=1, tiled=True)  9.96 us
    mul x2, local copies, waits for them, and re-layouts, apply_mask(): return (grid * keep).reshape(total, width, width)  9.92 us
    mul x1, other arithmetic, apply_mask(): return (grid * keep).reshape(total, width, width)  8.05 us
    reduce_sum x2, other arithmetic, update_cols(): jnp.sum(coef * coef)  6.78 us
    psum x2, blocking collectives, update_cols(): norm_sum = lax.psum(jnp.sum(moved * moved), 'col')  6.27 us
  transfers between devices with their start and end apart: 4, of which 3 were waited for; matrix products, arithmetic and copies ran while one was open for 6% of the time, Pallas kernels for 0%

commit v1 on v0

--- a/solution.py
+++ b/solution.py
@@ -44,7 +44,7 @@
             preferred_element_type=jnp.float32,
         ).astype(jnp.bfloat16)
         partial_sum = jnp.einsum("kab,kbc->ac", masked, inner, preferred_element_type=jnp.float32)
-        sigma = lax.psum(partial_sum, "op")
+        sigma = jnp.sum(lax.all_gather(partial_sum, "op"), axis=0)
         coef = update_cols(coef, sigma, diag_energy, cells)
     return coef
 

time: 311 us -> 579 us (1.86)
  waiting for transfers between devices: 218 us -> 467 us
  other arithmetic: 34.9 us -> 53.9 us
    all_gather x0 -> x2, waiting for transfers between devices: none -> 458 us  [local(): sigma = jnp.sum(lax.all_gather(partial_sum, 'op'), axis=0)]
    psum x2 -> x0, waiting for transfers between devices: 208 us -> none  [local(): sigma = lax.psum(partial_sum, 'op')]
    reduce_sum x0 -> x2, other arithmetic: none -> 18.8 us  [local(): sigma = jnp.sum(lax.all_gather(partial_sum, 'op'), axis=0)]
  transfers between devices with their start and end apart: 4 -> 4, of which waited for: 3 -> 3; matrix products, arithmetic and copies ran while one was open for 6% -> 3% of each run, Pallas kernels for 0% -> 0%
where the time goes in v1:
time: 579 us; the launch traced here: 578 us
  waiting for transfers between devices  467 us (81%)
  other arithmetic  53.9 us (9%)
  matrix products  17.4 us (3%)
  between operations  17 us (3%)
  blocking collectives  12.4 us (2%)
  local copies, waits for them, and re-layouts  9.93 us (2%)
    all_gather x2, waiting for transfers between devices, local(): sigma = jnp.sum(lax.all_gather(partial_sum, 'op'), axis=0)  458 us
    reduce_sum x2, other arithmetic, local(): sigma = jnp.sum(lax.all_gather(partial_sum, 'op'), axis=0)  18.8 us
    dot_general x2, matrix products, local(): jnp.einsum('kab,kbc->ac', masked, inner, preferred_element_type=jnp.float32)  17.4 us
  transfers between devices with their start and end apart: 4, of which 3 were waited for; matrix products, arithmetic and copies ran while one was open for 3% of the time, Pallas kernels for 0%

profile of v1, /device:TPU:0, one launch (start us, length us, event | category | flops | bytes accessed | tf_op | source)
XLA Modules:
  0.0 578.0 jit_solution(5763751404830579556)
XLA Ops:
  6.5 0.0 copy-start
  6.5 0.0 copy-start.1
  6.5 0.0 all-gather.7.cloned.1.call-start
  6.5 2.9 convert_element_type.22
  9.4 0.0 all-gather.7.cloned.1.call-update
  9.4 0.0 all-gather.11.cloned.1.call-start
  9.5 0.0 copy-done.1
  9.5 2.5 mul.65
  12.0 7.4 %mul.66 = bf16[2,1024,1024]{2,1,0:T(8,128)(2,1)} reshape(bf16[2,8,128,8,128]{4,3,2,1,0:T(8,128)(2,1)} %mul.65) | data formatting | bytes 8388608 | tf_op jit(solution)/shard_map/mul | solution.py:16
  19.4 8.0 %mul.67 = bf16[2,1024,1024]{2,1,0:T(8,128)(2,1)} multiply(bf16[2,1024,1024]{2,1,0:T(8,128)(2,1)} %param.7, bf16[2,1024,1024]{2,1,0:T(8,128)(2,1)} %mul.66) | non-fusion elementwise | flops 2097152 | bytes 12582912 | tf_op jit(solution)/shard_map/mul | solution.py:16
  27.4 0.0 all-gather.7.cloned.1.call-done
  27.4 0.0 copy-done
  27.4 8.7 %fusion.10 = f32[1024,512]{1,0:T(8,128)} fusion(bf16[2,1024,1024]{2,1,0:T(8,128)(2,1)} %mul.67, bf16[2,1024,512]{2,1,0:T(8,128)(2,1)S(1)} %copy-done, bf16[1024,1024]{1,0:T(8,128)(2,1)} %all-gather.7.cloned.1.call-done), kind=kOutput, calls=%fused_computation.19 | convolution fusion | flops 4296015872 | bytes 10485760 | tf_op jit(solution)/shard_map/kab,kbc->ac/dot_general | solution.py:46
  36.1 0.0 all-gather.11.cloned.1.call-update
  36.1 0.0 all-gather.9.cloned.1.call-start
  36.2 229.7 %all-gather.11.cloned.1.call-done = f32[8192,512]{1,0:T(8,128)} async-done(((f32[1024,512]{1,0:T(8,128)}), f32[8192,512]{1,0:T(8,128)}) %all-gather.11.cloned.1.call-update) | async-done | bytes 16777232 | tf_op jit(solution)/shard_map/all_gather | solution.py:47
  265.9 9.4 %reduce_sum.72 = f32[1024,512]{1,0:T(8,128)} reduce(f32[8,1024,512]{2,1,0:T(8,128)} %bitcast.36, f32[]{:T(128)} %constant.10.clone.1), dimensions={0}, to_apply=%region_0.0 | reduce | flops 3670016 | bytes 18874372 | tf_op jit(solution)/shard_map/reduce_sum | solution.py:47
  275.3 3.4 multiply_reduce_fusion.4
  278.7 3.1 all-reduce.1
  283.2 5.7 multiply_reduce_fusion.3
  288.9 3.1 psum.44
  292.5 2.8 multiply_convert_fusion
  295.4 0.0 all-gather.9.cloned.1.call-update
  295.4 0.2 all-gather.13.cloned.1.call-start
  295.6 8.7 %all-gather.9.cloned.1.call-done = bf16[1024,1024]{1,0:T(8,128)(2,1)} async-done(((bf16[1024,512]{1,0:T(8,128)(2,1)}), bf16[1024,1024]{1,0:T(8,128)(2,1)}) %all-gather.9.cloned.1.call-update) | async-done | bytes 2097168 | tf_op jit(solution)/shard_map/all_gather | solution.py:42
  304.3 8.7 %fusion.13 = f32[1024,512]{1,0:T(8,128)} fusion(bf16[2,1024,1024]{2,1,0:T(8,128)(2,1)} %mul.67, bf16[2,1024,512]{2,1,0:T(8,128)(2,1)S(1)} %copy-done, bf16[1024,1024]{1,0:T(8,128)(2,1)} %all-gather.9.cloned.1.call-done), kind=kOutput, calls=%fused_computation.20 | convolution fusion | flops 4296015872 | bytes 10485760 | tf_op jit(solution)/shard_map/kab,kbc->ac/dot_general | solution.py:46
  313.0 0.0 all-gather.13.cloned.1.call-update
  313.0 228.6 %all-gather.13.cloned.1.call-done = f32[8192,512]{1,0:T(8,128)} async-done(((f32[1024,512]{1,0:T(8,128)}), f32[8192,512]{1,0:T(8,128)}) %all-gather.13.cloned.1.call-update) | async-done | bytes 16777232 | tf_op jit(solution)/shard_map/all_gather | solution.py:47
  541.6 9.4 %reduce_sum.76 = f32[1024,512]{1,0:T(8,128)} reduce(f32[8,1024,512]{2,1,0:T(8,128)} %bitcast.37, f32[]{:T(128)} %constant.10.clone.1), dimensions={0}, to_apply=%region_7.0 | reduce | flops 3670016 | bytes 18874372 | tf_op jit(solution)/shard_map/reduce_sum | solution.py:47
  551.1 3.4 multiply_reduce_fusion.1
  554.5 3.1 all-reduce
  559.0 5.7 multiply_reduce_fusion
  564.6 3.1 psum.47
  568.3 3.1 broadcast_multiply_fusion
  (1 shorter events, 0.0 us)
Async XLA Ops:
  6.5 20.9 %copy-start = (bf16[2,1024,512]{2,1,0:T(8,128)(2,1)S(1)}, bf16[2,1024,512]{2,1,0:T(8,128)(2,1)}, u32[]{:S(2)}) copy-start(bf16[2,1024,512]{2,1,0:T(8,128)(2,1)} %param.8) | copy-start | bytes 6291460
  6.5 2.9 copy-start.1
  6.5 20.9 %all-gather.7.cloned.1.call-start = ((), (), s32[]{:S(2)}) async-start(), calls=%async_computation | async-start | bytes 3145728 | tf_op jit(solution)/shard_map/all_gather | solution.py:42
  9.4 256.5 %all-gather.11.cloned.1.call-start = ((), (), s32[]{:S(2)}) async-start(), calls=%async_computation.2 | async-start | bytes 18874368 | tf_op jit(solution)/shard_map/all_gather | solution.py:47
  36.1 268.2 %all-gather.9.cloned.1.call-start = ((), (), s32[]{:S(2)}) async-start(), calls=%async_computation.1 | async-start | bytes 3145728 | tf_op jit(solution)/shard_map/all_gather | solution.py:42
  295.4 246.2 %all-gather.13.cloned.1.call-start = ((), (), s32[]{:S(2)}) async-start(), calls=%async_computation.3 | async-start | bytes 18874368 | tf_op jit(solution)/shard_map/all_gather | solution.py:47
Sparse Core Ops, SparseCore 0:
  9.5 13.2 all-gather.6
  36.2 229.5 all-gather.10
  295.5 8.7 all-gather.8
  313.1 228.4 all-gather.12
